TPU v7x, 256 devices: a whole 4x4x8 slice. The times are simulated.
256 devices in a mesh: dp: 2 (over y_hi), pipe: 16 (over y_lo, x, core), seq: 8 (over z).
Axes of the slice: x: 4, y: 4 (y_hi: 2, y_lo: 2; y = y_hi * 2 + y_lo), z: 8, core: 2. Of those that a mesh axis runs over, the one named last changes fastest.
Arguments:
- enc_out: bfloat16 [2, 512, 4096], P('dp', None, 'seq'), may hold values from -60 to 60
- w_key: bfloat16 [16, 4096, 2048], P('pipe', None, 'seq'), may hold values from -0.125 to 0.125
- w_value: bfloat16 [16, 4096, 2048], P('pipe', None, 'seq'), may hold values from -0.125 to 0.125
- query: bfloat16 [16, 2, 512, 2048], P('pipe', 'dp', None, 'seq'), may hold values from -256 to 256
- key_cache: bfloat16 [16, 2, 512, 2048], P('pipe', 'dp', None, 'seq'), may hold values from -6 to 6
- value_cache: bfloat16 [16, 2, 512, 2048], P('pipe', 'dp', None, 'seq'), may hold values from -6 to 6
- grad_attn: bfloat16 [16, 2, 512, 2048], P('pipe', 'dp', None, 'seq'), may hold values from -200 to 200
- dec_segments: int32 [2, 512], P('dp'), may hold values from 0 to 3, as said below
- enc_segments: int32 [2, 512], P('dp'), may hold values from 0 to 3, as said below
Outputs:
- grad_query: bfloat16 [16, 2, 512, 2048], P('pipe', 'dp', None, 'seq')
- grad_enc: float32 [2, 512, 4096], P('dp', 'seq', 'pipe')
- grad_wkey: float32 [16, 4096, 2048], P('pipe', 'dp', 'seq')
- grad_wvalue: float32 [16, 4096, 2048], P('pipe', 'dp', 'seq')
Inputs may be any that keep to these rules, and one draw needn't show every extreme that they name: `dec_segments`: never falling along a sequence; every number from 0 to 3 occurs; a segment holds 1 to 256 tokens, and one holds exactly 256. `enc_segments`: never falling along a sequence; every number from 0 to 3 occurs; a segment holds 1 to 256 tokens, and one holds exactly 256.
All inputs are finite; a program needn't handle non-finite values.
Results may differ from a plain program's by a relative error of at most 0.006.
Values may be sent and summed in bfloat16 or wider, within the bound.
No kernel may reach another device: no remote copies, remote signals or barrier semaphores. Data moves between devices by JAX's collectives and lax.ppermute only.
A program may use at most 128 MiB of HBM per device.

v0:
```python
import math

import jax
import jax.numpy as jnp
from jax import lax
from jax.experimental import pallas as pl
from jax.experimental.pallas import tpu as pltpu
from jax.sharding import PartitionSpec as P


D = 4096
H = 8
HD = 256


F32 = jnp.float32
BF16 = jnp.bfloat16
LAST = (((1,), (1,)), ((), ()))
FIRST = (((0,), (0,)), ((), ()))
PLAIN = (((1,), (0,)), ((), ()))
VM = pltpu.VMEM
HB = pltpu.HBM
DMA = pltpu.SemaphoreType.DMA
MIB = 1 << 20
FULL = 63
ATTN = 54
X1, X3, Y1 = (0, 1), (0, 3), (1, 0)
ORDERS = ((X1, X3, Y1), (X3, X1, Y1))
RANGES = (256, 256)
NEAR = (0, -1, 1, -2, 2)
FAR = (-3, 3, 4, 4)


def dot(a, b, dims):
    return lax.dot_general(a, b, dims, preferred_element_type=F32)


def call(kernel, out, ins, spaces, outs=None, scratch=(), limit=12, flops=0, size=0, alias=None):
    outs = outs or (VM,) * len(out)
    return pl.pallas_call(
        kernel,
        out_shape=out,
        in_specs=[pl.BlockSpec(memory_space=m) for m in spaces],
        out_specs=tuple(pl.BlockSpec(memory_space=m) for m in outs),
        scratch_shapes=list(scratch),
        input_output_aliases=alias or {},
        compiler_params=pltpu.CompilerParams(vmem_limit_bytes=limit * MIB),
        cost_estimate=pl.CostEstimate(flops=flops, bytes_accessed=size, transcendentals=0),
    )(*ins)


def place():
    at = lax.axis_index("pipe")
    core = lax.rem(at, 2)
    x = lax.rem(lax.div(at, 2), 4)
    low = lax.div(at, 8)
    return low, x, core


def half_kernel(enc_ref, out_ref, block, sem):
    _, _, core = place()
    start = pl.multiple_of(core * 256, 256)
    copy = pltpu.make_async_copy(enc_ref.at[0, :, pl.ds(start, 256)], block, sem)
    copy.start()
    copy.wait()
    out_ref[...] = block[...].astype(F32).T.astype(BF16)


def attention_kernel(
    dec_hbm, enc_hbm, q_hbm, k_hbm, v_hbm, g_hbm, gq_ref, both_ref, dec, enc, qs, ks, vs, gs, sems
):
    inverse_root = 1.0 / math.sqrt(HD)
    copies = [
        pltpu.make_async_copy(src, dst, sems.at[i])
        for i, (src, dst) in enumerate(
            (
                (k_hbm.at[0, 0], ks),
                (q_hbm.at[0, 0], qs),
                (dec_hbm, dec),
                (enc_hbm, enc),
                (v_hbm.at[0, 0], vs),
                (g_hbm.at[0, 0], gs),
            )
        )
    ]
    for copy in copies:
        copy.start()
    for copy in copies[:4]:
        copy.wait()
    q = qs[...]
    k = ks[...]
    length = q.shape[0]
    column = jnp.broadcast_to(enc[...].astype(F32), (128, length)).T[:, :1]
    scores = dot(k, q, LAST) * inverse_root
    scores = jnp.where(column == dec[...].astype(F32), scores, -jnp.inf)
    exps = jnp.exp(scores - jnp.max(scores, axis=0, keepdims=True))
    probs = exps / jnp.sum(exps, axis=0, keepdims=True)
    for copy in copies[4:]:
        copy.wait()
    g = gs[...]
    dprobs = dot(vs[...], g, LAST)
    delta = jnp.sum(probs * dprobs, axis=0, keepdims=True)
    dscores = (probs * (dprobs - delta) * inverse_root).astype(BF16)
    both_ref[:, :HD] = dot(dscores, q, PLAIN).astype(BF16)
    both_ref[:, HD:] = dot(probs.astype(BF16), g, PLAIN).astype(BF16)
    gq_ref[0, 0] = dot(dscores, k, FIRST).astype(BF16)


def both_of(a, b):
    return (a[0] ^ b[0], a[1] ^ b[1])


def terms(both_ref, wk_ref, wv_ref, bit, use):
    low, x, _ = place()
    for m in (1, 2, 3, 0):
        for n in range(2):
            block = (jnp.bitwise_xor(low, n) * 4 + jnp.bitwise_xor(x, m)) * 2 + bit
            rows = pl.ds(pl.multiple_of(block * 256, 256), 256)
            value = dot(both_ref[:, :HD], wk_ref[0, rows, :], LAST)
            use(m, n, value + dot(both_ref[:, HD:], wv_ref[0, rows, :], LAST))


def other_core_kernel(both_ref, wk_ref, wv_ref, out_ref, copy_ref):
    _, _, core = place()

    def use(m, n, value):
        out_ref[m, n] = value.astype(BF16)

    copy_ref[...] = both_ref[...]
    terms(both_ref, wk_ref, wv_ref, 1 - core, use)


def own_core_kernel(both_ref, wk_ref, wv_ref, got_ref, *outs):
    _, _, core = place()

    def use(m, n, value):
        total = value + got_ref[m, n].astype(F32)
        at = 0
        for i, count in enumerate(RANGES):
            first, second, third = ORDERS[i]
            kept = [(0, 0), third, second, both_of(second, third)]
            part = total[at : at + count]
            at += count
            if (n, m) in kept:
                outs[2 * i + 1][kept.index((n, m))] = part
            else:
                outs[2 * i][kept.index(both_of((n, m), first))] = part.astype(BF16)

    terms(both_ref, wk_ref, wv_ref, core, use)


def accumulate(total, grads, steps, own, other):
    d = lax.axis_index("dp")
    z = lax.axis_index("seq")
    _, _, core = place()
    for i, step in enumerate(steps):
        u = lax.rem(z + step - 4 * d + 16, 8)
        which = lax.div(u, 4)
        chunk = jnp.where(u < 4, u, lax.rem(u + 2, 4))
        grad = grads[which]
        for refs_of, bit in ((own, core), (other, 1 - core)):
            piece = refs_of[i][...]
            start = chunk * 512 + bit * 256
            if i and steps[i - 1] == step:
                start = start + 128
            rows = pl.ds(pl.multiple_of(start, 128), piece.shape[0])
            total[rows, :] += dot(piece, grad, PLAIN)


def near_kernel(*refs):
    count = len(NEAR)
    own, other = refs[:count], refs[count : 2 * count]
    here_ref, there_ref, total, grads = refs[2 * count :]
    grads[0] = here_ref[...]
    grads[1] = there_ref[...]
    total[...] = jnp.zeros_like(total)
    accumulate(total, grads, NEAR, own, other)


def far_kernel(*refs):
    count = len(FAR)
    own, other = refs[:count], refs[count : 2 * count]
    here_ref, there_ref, _, total, square_ref, grads = refs[2 * count :]
    grads[0] = here_ref[...]
    grads[1] = there_ref[...]
    accumulate(total, grads, FAR, own, other)
    square_ref[...] = jnp.zeros_like(square_ref)
    for i in range(2):
        value = total[:, i * HD : (i + 1) * HD]
        square = jnp.sum(value * value, axis=0, keepdims=True)
        square_ref[0:1, i * 128 : (i + 1) * 128] = square[:, :128] + square[:, 128:]


def encode(row):
    high = row.astype(BF16).astype(F32)
    middle = (row - high).astype(BF16).astype(F32)
    low = row - high - middle
    line = lax.broadcasted_iota(jnp.int32, (16, 256), 0)
    tile = jnp.where(line == 1, middle, jnp.where(line == 2, low, 0.0))
    return jnp.where(line == 0, high, tile).astype(BF16)


def decode(tile):
    return jnp.sum(tile.astype(F32), axis=0, keepdims=True)


def pack_kernel(*refs):
    first_ref, second_ref, came_ref, here_ref, there_ref = refs[:5]
    up_ref, down_ref, keep_ref, square_ref, whole = refs[5:]
    z = lax.axis_index("seq")
    whole[:256, :] = first_ref[0] + came_ref[:256, :].astype(F32)
    whole[256:, :] = second_ref[0] + came_ref[256:, :].astype(F32)
    for ref, places in ((up_ref, (2, 3, 4)), (down_ref, (-3, -2)), (keep_ref, (-1, 0, 1))):
        for i, by in enumerate(places):
            start = pl.multiple_of(lax.rem(z + by + 8, 8) * 64, 64)
            ref[i * 64 : (i + 1) * 64, :] = whole[pl.ds(start, 64), :].astype(ref.dtype)
    square_ref[...] = here_ref[...] + there_ref[...]
    tile = encode(square_ref[0:1, :])
    up_ref[192:, :] = tile
    down_ref[128:, :] = tile


def middle_kernel(
    keep_ref, square_ref, up_ref, down_ref, last_ref, next_ref, keep_out, square_out
):
    up = up_ref[:192, :].astype(F32)
    down = down_ref[:128, :].astype(F32)
    keep = keep_ref[...]
    last_ref[:64, :] = (keep[:64] + up[:64]).astype(BF16)
    next_ref[:64, :] = (keep[128:] + up[128:] + down[64:]).astype(BF16)
    keep_out[...] = keep[64:128] + up[64:128] + down[:64]
    behind = square_ref[0:1, :] + decode(up_ref[192:, :])
    around = behind + decode(down_ref[128:, :])
    square_out[...] = jnp.broadcast_to(around, square_out.shape)
    last_ref[64:, :] = encode(behind)
    next_ref[64:, :] = encode(around)


def finish_kernel(
    keep_ref,
    around_ref,
    last_ref,
    next_ref,
    total,
    enc_ref,
    key_ref,
    value_ref,
    scaled,
    enc,
    sems,
):
    enc[...] = keep_ref[...] + last_ref[:64, :].astype(F32) + next_ref[:64, :].astype(F32)
    copies = [pltpu.make_async_copy(enc, enc_ref.at[0], sems.at[2, 0])]
    copies[0].start()
    squares = around_ref[0:1, :] + decode(last_ref[64:, :]) + decode(next_ref[64:, :])
    for i, ref in enumerate((key_ref, value_ref)):
        square = jnp.sum(squares[:, i * 128 : (i + 1) * 128], axis=1, keepdims=True)
        factor = 1.0 / jnp.sqrt(square / (D * H * HD) + 1e-06)
        for j in range(4):
            rows = slice(j * 512, (j + 1) * 512)
            scaled[i, rows, :] = total[rows, i * HD : (i + 1) * HD] * factor
            copy = pltpu.make_async_copy(
                scaled.at[i, rows, :], ref.at[0, rows, :], sems.at[i, j]
            )
            copy.start()
            copies.append(copy)
    for copy in copies:
        copy.wait()


def shards(
    enc_out, w_key, w_value, query, key_cache, value_cache, grad_attn, dec_segments, enc_segments
):
    length = query.shape[2]
    columns = query.shape[3]
    shape = jax.ShapeDtypeStruct

    def shift(value, by):
        return lax.ppermute(value, "seq", [(i, (i + by) % 8) for i in range(8)])

    def swap(value, low, x, core):
        mask = low * 8 + x * 2 + core
        return lax.ppermute(value, "pipe", [(i, i ^ mask) for i in range(16)])

    (piece,) = call(
        half_kernel,
        (shape((256, length), BF16),),
        (enc_out,),
        (HB,),
        scratch=(VM((length, 256), BF16), DMA),
        limit=FULL,
        size=MIB,
    )
    pairs = []
    for b in range(2):
        for z in range(8):
            to = (z + 2) % 8 if z in (2, 3, 6, 7) else (z - 2) % 8
            inside = z // 4 == b
            pairs.append((b * 8 + z, b * 8 + z if inside else (1 - b) * 8 + to))
    held = lax.ppermute(piece, ("dp", "seq"), pairs)

    line = VM((length, columns), BF16)
    grad_query, both = call(
        attention_kernel,
        (shape((1, 1, length, columns), BF16), shape((length, 2 * columns), BF16)),
        (dec_segments, enc_segments, query, key_cache, value_cache, grad_attn),
        (HB,) * 6,
        scratch=(VM((1, length), jnp.int32),) * 2 + (line,) * 4 + (DMA((6,)),),
        limit=ATTN,
        flops=5 * 2 * 512 * 512 * 256,
        size=2 * MIB,
    )
    sent, both = call(
        other_core_kernel,
        (shape((4, 2, length, 256), BF16), shape((length, 2 * columns), BF16)),
        (both, w_key, w_value),
        (VM,) * 3,
        limit=8,
        flops=1 << 30,
        size=5 * MIB,
    )
    there = lax.ppermute(both, "dp", [(0, 1), (1, 0)])
    got = swap(sent, 0, 0, 1)

    ahead = [held] + [shift(held, k) for k in (1, 2)]
    behind = [held] + [shift(held, -k) for k in (1, 2)]
    ahead.append(shift(ahead[2], 1))
    behind.append(shift(behind[2], -1))
    far = (shift(ahead[2][:128], 2), shift(behind[2][128:], -2))

    out = []
    for count in RANGES:
        out += [shape((4, count, 256), BF16), shape((4, count, 256), F32)]
    out = call(
        own_core_kernel,
        tuple(out),
        (both, w_key, w_value, got),
        (VM,) * 4,
        limit=8,
        flops=1 << 30,
        size=8 * MIB,
    )
    kept = [out[2 * i + 1] for i in range(2)]
    sent = [out[2 * i] for i in range(2)]
    for stage in range(2):
        came = [
            swap(sent[i], ORDERS[i][stage][0], ORDERS[i][stage][1], 0)
            for i in range(2)
        ]
        total = [kept[i] + came[i].astype(F32) for i in range(2)]
        half = 2 - stage
        kept = [value[:half] for value in total]
        sent = [value[half:].astype(BF16) for value in total]
    came = swap(jnp.concatenate(sent, axis=1)[0], 1, 0, 0)

    own = [held, ahead[1], behind[1], ahead[2], behind[2]]
    other = [swap(value, 0, 0, 1) for value in own]
    grads = VM((2, length, 2 * HD), BF16)
    sums = shape((2048, 2 * HD), F32)
    (total,) = call(
        near_kernel,
        (sums,),
        (*own, *other, both, there),
        (VM,) * 12,
        scratch=(grads,),
        limit=8,
        flops=5 << 28,
        size=8 * MIB,
    )
    own = [ahead[3], behind[3], *far]
    other = [swap(value, 0, 0, 1) for value in own]
    total, square = call(
        far_kernel,
        (sums, shape((8, 256), F32)),
        (*own, *other, both, there, total),
        (VM,) * 11,
        scratch=(grads,),
        limit=8,
        flops=3 << 28,
        size=8 * MIB,
        alias={10: 0},
    )
    square_there = lax.ppermute(square, "dp", [(0, 1), (1, 0)])
    up, down, keep, square = call(
        pack_kernel,
        (
            shape((208, 256), BF16),
            shape((144, 256), BF16),
            shape((192, 256), F32),
            shape((8, 256), F32),
        ),
        (*kept, came, square, square_there),
        (VM,) * 5,
        scratch=(VM((length, 256), F32),),
        limit=4,
        size=2 * MIB,
    )
    up = shift(up, 3)
    down = shift(down, -3)
    last, following, keep, square = call(
        middle_kernel,
        (
            shape((80, 256), BF16),
            shape((80, 256), BF16),
            shape((64, 256), F32),
            shape((8, 256), F32),
        ),
        (keep, square, up, down),
        (VM,) * 4,
        limit=4,
        size=MIB,
    )
    last = shift(last, -1)
    following = shift(following, 1)
    grad_enc, grad_wkey, grad_wvalue = call(
        finish_kernel,
        (shape((1, 64, 256), F32), *(shape((1, 2048, HD), F32),) * 2),
        (keep, square, last, following, total),
        (VM,) * 5,
        outs=(HB, HB, HB),
        scratch=(VM((2, 2048, HD), F32), VM((64, 256), F32), DMA((3, 4))),
        limit=12,
        size=8 * MIB,
    )
    return (grad_query, grad_enc, grad_wkey, grad_wvalue)


def solution(mesh):
    in_specs = (
        P("dp", None, "seq"),
        P("pipe", None, "seq"),
        P("pipe", None, "seq"),
        P("pipe", "dp", None, "seq"),
        P("pipe", "dp", None, "seq"),
        P("pipe", "dp", None, "seq"),
        P("pipe", "dp", None, "seq"),
        P("dp", None),
        P("dp", None),
    )
    out_specs = (
        P("pipe", "dp", None, "seq"),
        P("dp", "seq", "pipe"),
        P("pipe", "dp", "seq"),
        P("pipe", "dp", "seq"),
    )
    return jax.shard_map(
        shards, mesh=mesh, in_specs=in_specs, out_specs=out_specs, check_vma=False
    )
```

profile of v0, /device:TPU:4, one launch (start us, length us, event | category | flops | bytes accessed | tf_op | source)
XLA Modules:
  0.0 108.2 jit_solution(14550937197814504)
XLA Ops:
  0.6 3.7 %shard_map.120 = (bf16[1,1,512,256]{3,2,1,0:T(8,128)(2,1)}, bf16[512,512]{1,0:T(8,128)(2,1)}) custom-call(s32[1,512]{1,0:T(1,128)} %dec_hbm.1, s32[1,512]{1,0:T(1,128)} %enc_hbm.1, bf16[1,1,512,256]{3,2,1,0:T(8,128)(2,1)} %q_hbm.1, bf16[1,1,512,256]{3,2,1,0:T(8,128)(2,1)} %k_hbm.1, bf16[1,1,512,256]{3,2,1,0:T(8,128)(2,1)} %v_hbm.1, ...), custom_call_target="tpu_custom_call" | custom-call | flops 671088640 | bytes 2097152 | tf_op jit(solution)/shard_map/pallas_call | solution.py:40
  7.0 2.6 %shard_map.121 = (bf16[4,2,512,256]{3,2,1,0:T(8,128)(2,1)}, bf16[512,512]{1,0:T(8,128)(2,1)S(1)}) custom-call(bf16[512,512]{1,0:T(8,128)(2,1)S(1)} %copy-done.4, bf16[1,4096,256]{2,1,0:T(8,128)(2,1)S(1)} %copy-done, bf16[1,4096,256]{2,1,0:T(8,128)(2,1)S(1)} %copy-done.2), custom_call_target="tpu_custom_call" | custom-call | flops 1073741824 | bytes 5242880 | tf_op jit(solution)/shard_map/pallas_call | solution.py:40
  9.7 1.8 %shard_map.123 = bf16[256,512]{1,0:T(8,128)(2,1)} custom-call(bf16[1,512,512]{2,1,0:T(8,128)(2,1)} %enc_ref.1), custom_call_target="tpu_custom_call" | custom-call | bytes 1048576 | tf_op jit(solution)/shard_map/pallas_call | solution.py:40
  11.5 1.6 %collective-permute-start.6 = (bf16[256,512]{1,0:T(8,128)(2,1)}, bf16[256,512]{1,0:T(8,128)(2,1)S(1)}, u32[]{:S(2)}, u32[]{:S(2)}) collective-permute-start(bf16[256,512]{1,0:T(8,128)(2,1)} %shard_map.123), channel_id=1, source_target_pairs={{0,0},{1,1},{2,2},{3,3},{4,130},{5,131},{6,128},{7,129},{128,6},{1... | collective-permute-start | bytes 786440 | tf_op jit(solution)/shard_map/ppermute | solution.py:300
  14.2 1.6 %copy-done.1 = bf16[1,4096,256]{2,1,0:T(8,128)(2,1)S(1)} copy-done((bf16[1,4096,256]{2,1,0:T(8,128)(2,1)S(1)}, bf16[1,4096,256]{2,1,0:T(8,128)(2,1)}, u32[]{:S(2)}) %copy-start.1) | copy-done | bytes 2097176
  17.3 2.9 %shard_map.122 = (bf16[4,256,256]{2,1,0:T(8,128)(2,1)S(1)}, f32[4,256,256]{2,1,0:T(8,128)S(1)}, bf16[4,256,256]{2,1,0:T(8,128)(2,1)S(1)}, f32[4,256,256]{2,1,0:T(8,128)S(1)}) custom-call(bf16[512,512]{1,0:T(8,128)(2,1)S(1)} %get-tuple-element.27.both_ref.refs_10_.refs_8_, bf16[1,4096,256]{2,1,0:T(8,128)(2,1)S(1)} %copy-done.1, ...), custom_call_target="tpu_custom_call" | custom-call | flops 1073741824 | bytes 8388608 | tf_op jit(solution)/shard_map/pallas_call | solution.py:40
  21.5 3.3 %collective-permute-start.7 = (bf16[256,512]{1,0:T(8,128)(2,1)S(1)}, bf16[256,512]{1,0:T(8,128)(2,1)S(1)}, u32[]{:S(2)}, u32[]{:S(2)}) collective-permute-start(bf16[256,512]{1,0:T(8,128)(2,1)S(1)} %collective-permute-done.6.refs_0_), channel_id=1, source_target_pairs={{0,2},{1,3},{2,4},{3,5},{4,6},{5,7},{6,0},{7,1},{8,10},{9,11},{10,... | collective-permute-start | bytes 786440 | tf_op jit(solution)/shard_map/ppermute | solution.py:279
  24.8 14.1 %collective-permute-start.17 = (bf16[512,512]{1,0:T(8,128)(2,1)S(1)}, bf16[512,512]{1,0:T(8,128)(2,1)S(1)}, u32[]{:S(2)}, u32[]{:S(2)}) collective-permute-start(bf16[512,512]{1,0:T(8,128)(2,1)S(1)} %get-tuple-element.27.both_ref.refs_10_.refs_8_), channel_id=1, source_target_pairs={{0,128},{128,0},{1,129},{129,1},{2,130},{130,2},{3,131},{131,3},{4... | collective-permute-start | bytes 1572872 | tf_op jit(solution)/shard_map/ppermute | solution.py:322
  39.5 11.0 %collective-permute-done.7.refs_3_ = bf16[256,512]{1,0:T(8,128)(2,1)S(1)} collective-permute-done((bf16[256,512]{1,0:T(8,128)(2,1)S(1)}, bf16[256,512]{1,0:T(8,128)(2,1)S(1)}, u32[]{:S(2)}, u32[]{:S(2)}) %collective-permute-start.7) | collective-permute-done | bytes 262176 | tf_op jit(solution)/shard_map/ppermute | solution.py:279
  50.5 3.3 %collective-permute-start.19 = (bf16[256,512]{1,0:T(8,128)(2,1)S(1)}, bf16[256,512]{1,0:T(8,128)(2,1)S(1)}, u32[]{:S(2)}, u32[]{:S(2)}) collective-permute-start(bf16[256,512]{1,0:T(8,128)(2,1)S(1)} %collective-permute-done.6.refs_0_), channel_id=1, source_target_pairs={{0,7},{1,0},{2,1},{3,2},{4,3},{5,4},{6,5},{7,6},{8,15},{9,8},{10,9... | collective-permute-start | bytes 786440 | tf_op jit(solution)/shard_map/ppermute | solution.py:279
  55.2 8.4 %collective-permute-done.18.refs_1_ = bf16[256,512]{1,0:T(8,128)(2,1)S(1)} collective-permute-done((bf16[256,512]{1,0:T(8,128)(2,1)S(1)}, bf16[256,512]{1,0:T(8,128)(2,1)S(1)}, u32[]{:S(2)}, u32[]{:S(2)}) %collective-permute-start.18) | collective-permute-done | bytes 262176 | tf_op jit(solution)/shard_map/ppermute | solution.py:279
  65.8 2.5 %collective-permute-start.10 = (bf16[256,512]{1,0:T(8,128)(2,1)S(1)}, bf16[256,512]{1,0:T(8,128)(2,1)S(1)}, u32[]{:S(2)}, u32[]{:S(2)}) collective-permute-start(bf16[256,512]{1,0:T(8,128)(2,1)S(1)} %collective-permute-done.9.refs_4_), channel_id=1, source_target_pairs={{0,7},{1,0},{2,1},{3,2},{4,3},{5,4},{6,5},{7,6},{8,15},{9,8},{10,9... | collective-permute-start | bytes 786440 | tf_op jit(solution)/shard_map/ppermute | solution.py:279
  68.4 4.5 %collective-permute-done.12.refs_3_ = bf16[128,512]{1,0:T(8,128)(2,1)S(1)} collective-permute-done((bf16[128,512]{1,0:T(8,128)(2,1)S(1)}, bf16[128,512]{1,0:T(8,128)(2,1)S(1)}, u32[]{:S(2)}, u32[]{:S(2)}) %collective-permute-start.12) | collective-permute-done | bytes 131104 | tf_op jit(solution)/shard_map/ppermute | solution.py:279
  73.6 2.6 %collective-permute-done.10.refs_1_ = bf16[256,512]{1,0:T(8,128)(2,1)S(1)} collective-permute-done((bf16[256,512]{1,0:T(8,128)(2,1)S(1)}, bf16[256,512]{1,0:T(8,128)(2,1)S(1)}, u32[]{:S(2)}, u32[]{:S(2)}) %collective-permute-start.10) | collective-permute-done | bytes 262176 | tf_op jit(solution)/shard_map/ppermute | solution.py:279
  76.8 1.6 %collective-permute-start.5 = (bf16[512,256]{1,0:T(8,128)(2,1)S(1)}, bf16[512,256]{1,0:T(8,128)(2,1)S(1)}, u32[]{:S(2)}, u32[]{:S(2)}) collective-permute-start(bf16[512,256]{1,0:T(8,128)(2,1)S(1)} %maximum_bitcast_fusion), channel_id=1, source_target_pairs={{0,64},{8,72},{16,80},{24,88},{32,96},{40,104},{48,112},{56,120},{... | collective-permute-start | bytes 786440 | tf_op jit(solution)/shard_map/ppermute | solution.py:283
  78.9 1.8 %shard_map.124.refs_10_ = f32[2048,512]{1,0:T(8,128)S(1)} custom-call(bf16[256,512]{1,0:T(8,128)(2,1)S(1)} %collective-permute-done.6.refs_0_, bf16[256,512]{1,0:T(8,128)(2,1)S(1)} %collective-permute-done.18.refs_1_, bf16[256,512]{1,0:T(8,128)(2,1)S(1)} %collective-permute-done.19.refs_2_, bf16[256,512]{1,0:T(8,128)(2,1)S(1)} %collective-permute-done.7.refs_3_, ...), custom_call_target="tpu_custom_call" | custom-call | flops 1342177280 | bytes 8388608 | tf_op jit(solution)/shard_map/pallas_call | solution.py:40
  83.8 3.7 %collective-permute-done.25.refs_4_ = f32[8,256]{1,0:T(8,128)S(1)} collective-permute-done((f32[8,256]{1,0:T(8,128)S(1)}, f32[8,256]{1,0:T(8,128)S(1)}, u32[]{:S(2)}, u32[]{:S(2)}) %collective-permute-start.25) | collective-permute-done | bytes 8224 | tf_op jit(solution)/shard_map/ppermute | solution.py:383
  87.6 2.3 %collective-permute-start.26 = (bf16[208,256]{1,0:T(8,128)(2,1)S(1)}, bf16[208,256]{1,0:T(8,128)(2,1)S(1)}, u32[]{:S(2)}, u32[]{:S(2)}) collective-permute-start(bf16[208,256]{1,0:T(8,128)(2,1)S(1)} %get-tuple-element.36), channel_id=1, source_target_pairs={{0,3},{1,4},{2,5},{3,6},{4,7},{5,0},{6,1},{7,2},{8,11},{9,12},{10,... | collective-permute-start | bytes 319496 | tf_op jit(solution)/shard_map/ppermute | solution.py:279
  89.9 2.8 %collective-permute-start.27 = (bf16[144,256]{1,0:T(8,128)(2,1)S(1)}, bf16[144,256]{1,0:T(8,128)(2,1)S(1)}, u32[]{:S(2)}, u32[]{:S(2)}) collective-permute-start(bf16[144,256]{1,0:T(8,128)(2,1)S(1)} %get-tuple-element.37), channel_id=1, source_target_pairs={{0,5},{1,6},{2,7},{3,0},{4,1},{5,2},{6,3},{7,4},{8,13},{9,14},{10,... | collective-permute-start | bytes 221192 | tf_op jit(solution)/shard_map/ppermute | solution.py:279
  92.7 4.9 %collective-permute-done.27.down_ref = bf16[144,256]{1,0:T(8,128)(2,1)S(1)} collective-permute-done((bf16[144,256]{1,0:T(8,128)(2,1)S(1)}, bf16[144,256]{1,0:T(8,128)(2,1)S(1)}, u32[]{:S(2)}, u32[]{:S(2)}) %collective-permute-start.27) | collective-permute-done | bytes 73760 | tf_op jit(solution)/shard_map/ppermute | solution.py:279
  97.7 2.9 %collective-permute-start.28 = (bf16[80,256]{1,0:T(8,128)(2,1)S(1)}, bf16[80,256]{1,0:T(8,128)(2,1)S(1)}, u32[]{:S(2)}, u32[]{:S(2)}) collective-permute-start(bf16[80,256]{1,0:T(8,128)(2,1)S(1)} %get-tuple-element.40), channel_id=1, source_target_pairs={{0,7},{1,0},{2,1},{3,2},{4,3},{5,4},{6,5},{7,6},{8,15},{9,8},{10,9... | collective-permute-start | bytes 122888 | tf_op jit(solution)/shard_map/ppermute | solution.py:279
  100.6 1.7 %collective-permute-done.28.last_ref = bf16[80,256]{1,0:T(8,128)(2,1)S(1)} collective-permute-done((bf16[80,256]{1,0:T(8,128)(2,1)S(1)}, bf16[80,256]{1,0:T(8,128)(2,1)S(1)}, u32[]{:S(2)}, u32[]{:S(2)}) %collective-permute-start.28) | collective-permute-done | bytes 40992 | tf_op jit(solution)/shard_map/ppermute | solution.py:279
  102.3 3.5 %collective-permute-done.29.next_ref = bf16[80,256]{1,0:T(8,128)(2,1)S(1)} collective-permute-done((bf16[80,256]{1,0:T(8,128)(2,1)S(1)}, bf16[80,256]{1,0:T(8,128)(2,1)S(1)}, u32[]{:S(2)}, u32[]{:S(2)}) %collective-permute-start.29) | collective-permute-done | bytes 40992 | tf_op jit(solution)/shard_map/ppermute | solution.py:279
  105.8 2.2 %shard_map.128 = (f32[1,64,256]{2,1,0:T(8,128)}, f32[1,2048,256]{2,1,0:T(8,128)}, f32[1,2048,256]{2,1,0:T(8,128)}) custom-call(f32[64,256]{1,0:T(8,128)S(1)} %get-tuple-element.38.keep_ref, f32[8,256]{1,0:T(8,128)S(1)} %get-tuple-element.39.around_ref, bf16[80,256]{1,0:T(8,128)(2,1)S(1)} %collective-permute-done.28.last_ref, ...), custom_call_target="tpu_custom_call" | custom-call | bytes 8388608 | tf_op jit(solution)/shard_map/pallas_call | solution.py:40
  (68 shorter events, 15.6 us)
Async XLA Ops:
  11.5 10.1 %collective-permute-start.6 = (bf16[256,512]{1,0:T(8,128)(2,1)}, bf16[256,512]{1,0:T(8,128)(2,1)S(1)}, u32[]{:S(2)}, u32[]{:S(2)}) collective-permute-start(bf16[256,512]{1,0:T(8,128)(2,1)} %shard_map.123), channel_id=1, source_target_pairs={{0,0},{1,1},{2,2},{3,3},{4,130},{5,131},{6,128},{7,129},{128,6},{1... | collective-permute-start | bytes 786440 | tf_op jit(solution)/shard_map/ppermute | solution.py:300
  20.2 30.3 %collective-permute-start.1 = (bf16[4,256,256]{2,1,0:T(8,128)(2,1)S(1)}, bf16[4,256,256]{2,1,0:T(8,128)(2,1)S(1)}, u32[]{:S(2)}, u32[]{:S(2)}) collective-permute-start(bf16[4,256,256]{2,1,0:T(8,128)(2,1)S(1)} %get-tuple-element.30), channel_id=1, source_target_pairs={{0,16},{8,24},{16,0},{24,8},{32,48},{40,56},{48,32},{56,40},{64,80... | collective-permute-start | bytes 1572872 | tf_op jit(solution)/shard_map/ppermute | solution.py:283
  21.5 29.0 %collective-permute-start.7 = (bf16[256,512]{1,0:T(8,128)(2,1)S(1)}, bf16[256,512]{1,0:T(8,128)(2,1)S(1)}, u32[]{:S(2)}, u32[]{:S(2)}) collective-permute-start(bf16[256,512]{1,0:T(8,128)(2,1)S(1)} %collective-permute-done.6.refs_0_), channel_id=1, source_target_pairs={{0,2},{1,3},{2,4},{3,5},{4,6},{5,7},{6,0},{7,1},{8,10},{9,11},{10,... | collective-permute-start | bytes 786440 | tf_op jit(solution)/shard_map/ppermute | solution.py:279
  24.8 29.3 %collective-permute-start.17 = (bf16[512,512]{1,0:T(8,128)(2,1)S(1)}, bf16[512,512]{1,0:T(8,128)(2,1)S(1)}, u32[]{:S(2)}, u32[]{:S(2)}) collective-permute-start(bf16[512,512]{1,0:T(8,128)(2,1)S(1)} %get-tuple-element.27.both_ref.refs_10_.refs_8_), channel_id=1, source_target_pairs={{0,128},{128,0},{1,129},{129,1},{2,130},{130,2},{3,131},{131,3},{4... | collective-permute-start | bytes 1572872 | tf_op jit(solution)/shard_map/ppermute | solution.py:322
  38.9 15.3 %collective-permute-start.3 = (bf16[4,256,256]{2,1,0:T(8,128)(2,1)S(1)}, bf16[4,256,256]{2,1,0:T(8,128)(2,1)S(1)}, u32[]{:S(2)}, u32[]{:S(2)}) collective-permute-start(bf16[4,256,256]{2,1,0:T(8,128)(2,1)S(1)} %get-tuple-element.32), channel_id=1, source_target_pairs={{0,48},{8,56},{16,32},{24,40},{32,16},{40,24},{48,0},{56,8},{64,11... | collective-permute-start | bytes 1572872 | tf_op jit(solution)/shard_map/ppermute | solution.py:283
  39.4 14.6 %collective-permute-start.9 = (bf16[256,512]{1,0:T(8,128)(2,1)S(1)}, bf16[256,512]{1,0:T(8,128)(2,1)S(1)}, u32[]{:S(2)}, u32[]{:S(2)}) collective-permute-start(bf16[256,512]{1,0:T(8,128)(2,1)S(1)} %collective-permute-done.6.refs_0_), channel_id=1, source_target_pairs={{0,6},{1,7},{2,0},{3,1},{4,2},{5,3},{6,4},{7,5},{8,14},{9,15},{10,... | collective-permute-start | bytes 786440 | tf_op jit(solution)/shard_map/ppermute | solution.py:279
  50.5 13.2 %collective-permute-start.18 = (bf16[256,512]{1,0:T(8,128)(2,1)S(1)}, bf16[256,512]{1,0:T(8,128)(2,1)S(1)}, u32[]{:S(2)}, u32[]{:S(2)}) collective-permute-start(bf16[256,512]{1,0:T(8,128)(2,1)S(1)} %collective-permute-done.6.refs_0_), channel_id=1, source_target_pairs={{0,1},{1,2},{2,3},{3,4},{4,5},{5,6},{6,7},{7,0},{8,9},{9,10},{10,1... | collective-permute-start | bytes 786440 | tf_op jit(solution)/shard_map/ppermute | solution.py:279
  50.5 13.2 %collective-permute-start.19 = (bf16[256,512]{1,0:T(8,128)(2,1)S(1)}, bf16[256,512]{1,0:T(8,128)(2,1)S(1)}, u32[]{:S(2)}, u32[]{:S(2)}) collective-permute-start(bf16[256,512]{1,0:T(8,128)(2,1)S(1)} %collective-permute-done.6.refs_0_), channel_id=1, source_target_pairs={{0,7},{1,0},{2,1},{3,2},{4,3},{5,4},{6,5},{7,6},{8,15},{9,8},{10,9... | collective-permute-start | bytes 786440 | tf_op jit(solution)/shard_map/ppermute | solution.py:279
  54.0 10.9 %collective-permute-start.20 = (bf16[256,512]{1,0:T(8,128)(2,1)S(1)}, bf16[256,512]{1,0:T(8,128)(2,1)S(1)}, u32[]{:S(2)}, u32[]{:S(2)}) collective-permute-start(bf16[256,512]{1,0:T(8,128)(2,1)S(1)} %collective-permute-done.6.refs_0_), channel_id=1, source_target_pairs={{0,8},{8,0},{16,24},{24,16},{32,40},{40,32},{48,56},{56,48},{64,72... | collective-permute-start | bytes 786440 | tf_op jit(solution)/shard_map/ppermute | solution.py:283
  54.1 11.7 %collective-permute-start.11 = (bf16[128,512]{1,0:T(8,128)(2,1)S(1)}, bf16[128,512]{1,0:T(8,128)(2,1)S(1)}, u32[]{:S(2)}, u32[]{:S(2)}) collective-permute-start(bf16[128,512]{1,0:T(8,128)(2,1)S(1)} %slice.52), channel_id=1, source_target_pairs={{0,2},{1,3},{2,4},{3,5},{4,6},{5,7},{6,0},{7,1},{8,10},{9,11},{10,... | collective-permute-start | bytes 393224 | tf_op jit(solution)/shard_map/ppermute | solution.py:279
  54.2 14.1 %collective-permute-start.2 = (bf16[2,256,256]{2,1,0:T(8,128)(2,1)S(1)}, bf16[2,256,256]{2,1,0:T(8,128)(2,1)S(1)}, u32[]{:S(2)}, u32[]{:S(2)}) collective-permute-start(bf16[2,256,256]{2,1,0:T(8,128)(2,1)S(1)} %slice.61), channel_id=1, source_target_pairs={{0,48},{8,56},{16,32},{24,40},{32,16},{40,24},{48,0},{56,8},{64,11... | collective-permute-start | bytes 786440 | tf_op jit(solution)/shard_map/ppermute | solution.py:283
  63.7 9.2 %collective-permute-start.8 = (bf16[256,512]{1,0:T(8,128)(2,1)S(1)}, bf16[256,512]{1,0:T(8,128)(2,1)S(1)}, u32[]{:S(2)}, u32[]{:S(2)}) collective-permute-start(bf16[256,512]{1,0:T(8,128)(2,1)S(1)} %collective-permute-done.7.refs_3_), channel_id=1, source_target_pairs={{0,1},{1,2},{2,3},{3,4},{4,5},{5,6},{6,7},{7,0},{8,9},{9,10},{10,1... | collective-permute-start | bytes 786440 | tf_op jit(solution)/shard_map/ppermute | solution.py:279
  63.7 9.7 %collective-permute-start.4 = (bf16[2,256,256]{2,1,0:T(8,128)(2,1)S(1)}, bf16[2,256,256]{2,1,0:T(8,128)(2,1)S(1)}, u32[]{:S(2)}, u32[]{:S(2)}) collective-permute-start(bf16[2,256,256]{2,1,0:T(8,128)(2,1)S(1)} %slice.60), channel_id=1, source_target_pairs={{0,16},{8,24},{16,0},{24,8},{32,48},{40,56},{48,32},{56,40},{64,80... | collective-permute-start | bytes 786440 | tf_op jit(solution)/shard_map/ppermute | solution.py:283
  64.9 8.0 %collective-permute-start.12 = (bf16[128,512]{1,0:T(8,128)(2,1)S(1)}, bf16[128,512]{1,0:T(8,128)(2,1)S(1)}, u32[]{:S(2)}, u32[]{:S(2)}) collective-permute-start(bf16[128,512]{1,0:T(8,128)(2,1)S(1)} %slice.53), channel_id=1, source_target_pairs={{0,6},{1,7},{2,0},{3,1},{4,2},{5,3},{6,4},{7,5},{8,14},{9,15},{10,... | collective-permute-start | bytes 393224 | tf_op jit(solution)/shard_map/ppermute | solution.py:279
  65.8 10.4 %collective-permute-start.10 = (bf16[256,512]{1,0:T(8,128)(2,1)S(1)}, bf16[256,512]{1,0:T(8,128)(2,1)S(1)}, u32[]{:S(2)}, u32[]{:S(2)}) collective-permute-start(bf16[256,512]{1,0:T(8,128)(2,1)S(1)} %collective-permute-done.9.refs_4_), channel_id=1, source_target_pairs={{0,7},{1,0},{2,1},{3,2},{4,3},{5,4},{6,5},{7,6},{8,15},{9,8},{10,9... | collective-permute-start | bytes 786440 | tf_op jit(solution)/shard_map/ppermute | solution.py:279
  68.3 7.9 %collective-permute-start.21 = (bf16[256,512]{1,0:T(8,128)(2,1)S(1)}, bf16[256,512]{1,0:T(8,128)(2,1)S(1)}, u32[]{:S(2)}, u32[]{:S(2)}) collective-permute-start(bf16[256,512]{1,0:T(8,128)(2,1)S(1)} %collective-permute-done.18.refs_1_), channel_id=1, source_target_pairs={{0,8},{8,0},{16,24},{24,16},{32,40},{40,32},{48,56},{56,48},{64,72... | collective-permute-start | bytes 786440 | tf_op jit(solution)/shard_map/ppermute | solution.py:283
  72.9 5.5 %collective-permute-start.23 = (bf16[256,512]{1,0:T(8,128)(2,1)S(1)}, bf16[256,512]{1,0:T(8,128)(2,1)S(1)}, u32[]{:S(2)}, u32[]{:S(2)}) collective-permute-start(bf16[256,512]{1,0:T(8,128)(2,1)S(1)} %collective-permute-done.7.refs_3_), channel_id=1, source_target_pairs={{0,8},{8,0},{16,24},{24,16},{32,40},{40,32},{48,56},{56,48},{64,72... | collective-permute-start | bytes 786440 | tf_op jit(solution)/shard_map/ppermute | solution.py:283
  72.9 5.5 %collective-permute-start.24 = (bf16[256,512]{1,0:T(8,128)(2,1)S(1)}, bf16[256,512]{1,0:T(8,128)(2,1)S(1)}, u32[]{:S(2)}, u32[]{:S(2)}) collective-permute-start(bf16[256,512]{1,0:T(8,128)(2,1)S(1)} %collective-permute-done.9.refs_4_), channel_id=1, source_target_pairs={{0,8},{8,0},{16,24},{24,16},{32,40},{40,32},{48,56},{56,48},{64,72... | collective-permute-start | bytes 786440 | tf_op jit(solution)/shard_map/ppermute | solution.py:283
  76.8 10.7 %collective-permute-start.5 = (bf16[512,256]{1,0:T(8,128)(2,1)S(1)}, bf16[512,256]{1,0:T(8,128)(2,1)S(1)}, u32[]{:S(2)}, u32[]{:S(2)}) collective-permute-start(bf16[512,256]{1,0:T(8,128)(2,1)S(1)} %maximum_bitcast_fusion), channel_id=1, source_target_pairs={{0,64},{8,72},{16,80},{24,88},{32,96},{40,104},{48,112},{56,120},{... | collective-permute-start | bytes 786440 | tf_op jit(solution)/shard_map/ppermute | solution.py:283
  82.3 5.2 %collective-permute-start.25 = (f32[8,256]{1,0:T(8,128)S(1)}, f32[8,256]{1,0:T(8,128)S(1)}, u32[]{:S(2)}, u32[]{:S(2)}) collective-permute-start(f32[8,256]{1,0:T(8,128)S(1)} %get-tuple-element.33.refs_3_), channel_id=1, source_target_pairs={{0,128},{128,0},{1,129},{129,1},{2,130},{130,2},{3,131},{131,3},{4... | collective-permute-start | bytes 24584 | tf_op jit(solution)/shard_map/ppermute | solution.py:383
  87.6 10.0 %collective-permute-start.26 = (bf16[208,256]{1,0:T(8,128)(2,1)S(1)}, bf16[208,256]{1,0:T(8,128)(2,1)S(1)}, u32[]{:S(2)}, u32[]{:S(2)}) collective-permute-start(bf16[208,256]{1,0:T(8,128)(2,1)S(1)} %get-tuple-element.36), channel_id=1, source_target_pairs={{0,3},{1,4},{2,5},{3,6},{4,7},{5,0},{6,1},{7,2},{8,11},{9,12},{10,... | collective-permute-start | bytes 319496 | tf_op jit(solution)/shard_map/ppermute | solution.py:279
  89.9 7.7 %collective-permute-start.27 = (bf16[144,256]{1,0:T(8,128)(2,1)S(1)}, bf16[144,256]{1,0:T(8,128)(2,1)S(1)}, u32[]{:S(2)}, u32[]{:S(2)}) collective-permute-start(bf16[144,256]{1,0:T(8,128)(2,1)S(1)} %get-tuple-element.37), channel_id=1, source_target_pairs={{0,5},{1,6},{2,7},{3,0},{4,1},{5,2},{6,3},{7,4},{8,13},{9,14},{10,... | collective-permute-start | bytes 221192 | tf_op jit(solution)/shard_map/ppermute | solution.py:279
  97.7 4.6 %collective-permute-start.28 = (bf16[80,256]{1,0:T(8,128)(2,1)S(1)}, bf16[80,256]{1,0:T(8,128)(2,1)S(1)}, u32[]{:S(2)}, u32[]{:S(2)}) collective-permute-start(bf16[80,256]{1,0:T(8,128)(2,1)S(1)} %get-tuple-element.40), channel_id=1, source_target_pairs={{0,7},{1,0},{2,1},{3,2},{4,3},{5,4},{6,5},{7,6},{8,15},{9,8},{10,9... | collective-permute-start | bytes 122888 | tf_op jit(solution)/shard_map/ppermute | solution.py:279
  100.6 5.2 %collective-permute-start.29 = (bf16[80,256]{1,0:T(8,128)(2,1)S(1)}, bf16[80,256]{1,0:T(8,128)(2,1)S(1)}, u32[]{:S(2)}, u32[]{:S(2)}) collective-permute-start(bf16[80,256]{1,0:T(8,128)(2,1)S(1)} %get-tuple-element.41), channel_id=1, source_target_pairs={{0,1},{1,2},{2,3},{3,4},{4,5},{5,6},{6,7},{7,0},{8,9},{9,10},{10,1... | collective-permute-start | bytes 122888 | tf_op jit(solution)/shard_map/ppermute | solution.py:279
  (11 other events, 31.2 us)
where the time goes:
time: 109 us; the launch traced here: 108 us
  starting transfers between devices  42.5 us (39%)
  waiting for transfers between devices  41.6 us (38%)
  Pallas kernels  16.7 us (15%)
  local copies, waits for them, and re-layouts  5.96 us (5%)
    ppermute x12, waiting for transfers between devices, shift(): return lax.ppermute(value, 'seq', [(i, (i + by) % 8) for i in range(8)])  36.7 us
    ppermute x12, starting transfers between devices, shift(): return lax.ppermute(value, 'seq', [(i, (i + by) % 8) for i in range(8)])  18.1 us
    pallas_call x9, Pallas kernels, call(): pl.pallas_call(kernel, out_shape=out, in_specs=[pl.BlockSpec(memory_space...  16.7 us
    ppermute x1, starting transfers between devices, shards(): there = lax.ppermute(both, 'dp', [(0, 1), (1, 0)])  14.1 us
    ppermute x15, starting transfers between devices, swap(): return lax.ppermute(value, 'pipe', [(i, i ^ mask) for i in range(16)])  7.19 us
    unnamed x10, local copies, waits for them, and re-layouts  5.82 us
    ppermute x1, waiting for transfers between devices, shards(): square_there = lax.ppermute(square, 'dp', [(0, 1), (1, 0)])  3.73 us
  transfers between devices with their start and end apart: 30, of which 9 were waited for; matrix products, arithmetic and copies ran while one was open for 1% of the time, Pallas kernels for 7%

commit v1 on v0

--- a/solution.py
+++ b/solution.py
@@ -204,36 +204,39 @@
     return jnp.sum(tile.astype(F32), axis=0, keepdims=True)
 
 
-def pack_kernel(*refs):
-    first_ref, second_ref, came_ref, here_ref, there_ref = refs[:5]
-    up_ref, down_ref, keep_ref, square_ref, whole = refs[5:]
+def pack_kernel(first_ref, second_ref, came_ref, up_ref, down_ref, keep_ref, whole):
     z = lax.axis_index("seq")
     whole[:256, :] = first_ref[0] + came_ref[:256, :].astype(F32)
     whole[256:, :] = second_ref[0] + came_ref[256:, :].astype(F32)
-    for ref, places in ((up_ref, (2, 3, 4)), (down_ref, (-3, -2)), (keep_ref, (-1, 0, 1))):
+    for ref, places in ((up_ref, (1, -2)), (down_ref, (-1, -4, 2)), (keep_ref, (0, -3, 3))):
         for i, by in enumerate(places):
             start = pl.multiple_of(lax.rem(z + by + 8, 8) * 64, 64)
             ref[i * 64 : (i + 1) * 64, :] = whole[pl.ds(start, 64), :].astype(ref.dtype)
-    square_ref[...] = here_ref[...] + there_ref[...]
-    tile = encode(square_ref[0:1, :])
-    up_ref[192:, :] = tile
-    down_ref[128:, :] = tile
 
 
 def middle_kernel(
-    keep_ref, square_ref, up_ref, down_ref, last_ref, next_ref, keep_out, square_out
+    keep_ref,
+    up_ref,
+    down_ref,
+    square_ref,
+    behind_ref,
+    after_ref,
+    last_ref,
+    next_ref,
+    keep_out,
+    square_out,
 ):
-    up = up_ref[:192, :].astype(F32)
-    down = down_ref[:128, :].astype(F32)
+    up = up_ref[...].astype(F32)
+    down = down_ref[...].astype(F32)
     keep = keep_ref[...]
-    last_ref[:64, :] = (keep[:64] + up[:64]).astype(BF16)
-    next_ref[:64, :] = (keep[128:] + up[128:] + down[64:]).astype(BF16)
-    keep_out[...] = keep[64:128] + up[64:128] + down[:64]
-    behind = square_ref[0:1, :] + decode(up_ref[192:, :])
-    around = behind + decode(down_ref[128:, :])
+    keep_out[...] = keep[:64] + up[:64] + down[:64]
+    last_ref[:64, :] = (keep[64:128] + up[64:] + down[64:128]).astype(BF16)
+    next_ref[:64, :] = (keep[128:] + down[128:]).astype(BF16)
+    after = square_ref[0:1, :] + after_ref[0:1, :]
+    around = after + behind_ref[0:1, :]
     square_out[...] = jnp.broadcast_to(around, square_out.shape)
-    last_ref[64:, :] = encode(behind)
-    next_ref[64:, :] = encode(around)
+    last_ref[64:, :] = encode(around)
+    next_ref[64:, :] = encode(after)
 
 
 def finish_kernel(
@@ -381,22 +384,20 @@
         alias={10: 0},
     )
     square_there = lax.ppermute(square, "dp", [(0, 1), (1, 0)])
-    up, down, keep, square = call(
+    up, down, keep = call(
         pack_kernel,
-        (
-            shape((208, 256), BF16),
-            shape((144, 256), BF16),
-            shape((192, 256), F32),
-            shape((8, 256), F32),
-        ),
-        (*kept, came, square, square_there),
-        (VM,) * 5,
+        (shape((128, 256), BF16), shape((192, 256), BF16), shape((192, 256), F32)),
+        (*kept, came),
+        (VM,) * 3,
         scratch=(VM((length, 256), F32),),
         limit=4,
         size=2 * MIB,
     )
-    up = shift(up, 3)
-    down = shift(down, -3)
+    up = shift(up, 1)
+    down = shift(down, -1)
+    square = square + square_there
+    behind = shift(square, 1)
+    after = shift(square, -1)
     last, following, keep, square = call(
         middle_kernel,
         (
@@ -405,13 +406,13 @@
             shape((64, 256), F32),
             shape((8, 256), F32),
         ),
-        (keep, square, up, down),
-        (VM,) * 4,
+        (keep, up, down, square, behind, after),
+        (VM,) * 6,
         limit=4,
         size=MIB,
     )
-    last = shift(last, -1)
-    following = shift(following, 1)
+    last = shift(last, -3)
+    following = shift(following, 3)
     grad_enc, grad_wkey, grad_wvalue = call(
         finish_kernel,
         (shape((1, 64, 256), F32), *(shape((1, 2048, HD), F32),) * 2),

time: 109 us -> 122 us (1.12)
  starting transfers between devices: 42.5 us -> 51.5 us
  waiting for transfers between devices: 41.6 us -> 46.3 us
  Pallas kernels: 16.7 us -> 14.3 us
  other arithmetic: 0.41 us -> 1.73 us
    ppermute x15, waiting for transfers between devices: 1.12 us -> 16.2 us  [swap(): return lax.ppermute(value, 'pipe', [(i, i ^ mask) for i in range(16)])]
    ppermute x12 -> x14, starting transfers between devices: 18.1 us -> 32.8 us  [shift(): return lax.ppermute(value, 'seq', [(i, (i + by) % 8) for i in range(8)])]
    ppermute x12 -> x14, waiting for transfers between devices: 36.7 us -> 25.6 us  [shift(): return lax.ppermute(value, 'seq', [(i, (i + by) % 8) for i in range(8)])]
    ppermute x1, starting transfers between devices: 14.1 us -> 8.18 us  [shards(): there = lax.ppermute(both, 'dp', [(0, 1), (1, 0)])]
    pallas_call x9, Pallas kernels: 16.7 us -> 14.3 us  [call(): pl.pallas_call(kernel, out_shape=out, in_specs=[pl.BlockSpec(memory_space...]
    add x4, other arithmetic: 0.39 us -> 1.71 us  [shards(): total = [kept[i] + came[i].astype(F32) for i in range(2)]]
    unnamed x10 -> x14, local copies, waits for them, and re-layouts: 5.82 us -> 5.36 us
  transfers between devices with their start and end apart: 30 -> 32, of which waited for: 9 -> 10; matrix products, arithmetic and copies ran while one was open for 1% -> 2% of each run, Pallas kernels for 7% -> 4%
where the time goes in v1:
time: 122 us; the launch traced here: 120 us
  starting transfers between devices  51.5 us (42%)
  waiting for transfers between devices  46.3 us (38%)
  Pallas kernels  14.3 us (12%)
  local copies, waits for them, and re-layouts  5.51 us (5%)
  other arithmetic  1.73 us (1%)
    ppermute x14, starting transfers between devices, shift(): return lax.ppermute(value, 'seq', [(i, (i + by) % 8) for i in range(8)])  32.8 us
    ppermute x14, waiting for transfers between devices, shift(): return lax.ppermute(value, 'seq', [(i, (i + by) % 8) for i in range(8)])  25.6 us
    ppermute x15, waiting for transfers between devices, swap(): return lax.ppermute(value, 'pipe', [(i, i ^ mask) for i in range(16)])  16.2 us
    pallas_call x9, Pallas kernels, call(): pl.pallas_call(kernel, out_shape=out, in_specs=[pl.BlockSpec(memory_space...  14.3 us
    ppermute x1, starting transfers between devices, shards(): there = lax.ppermute(both, 'dp', [(0, 1), (1, 0)])  8.18 us
    ppermute x15, starting transfers between devices, swap(): return lax.ppermute(value, 'pipe', [(i, i ^ mask) for i in range(16)])  8.11 us
    unnamed x14, local copies, waits for them, and re-layouts  5.36 us
    ppermute x1, waiting for transfers between devices, shards(): square_there = lax.ppermute(square, 'dp', [(0, 1), (1, 0)])  4.55 us
  transfers between devices with their start and end apart: 32, of which 10 were waited for; matrix products, arithmetic and copies ran while one was open for 2% of the time, Pallas kernels for 4%

profile of v1, /device:TPU:4, one launch (start us, length us, event | category | flops | bytes accessed | tf_op | source)
XLA Modules:
  0.0 120.4 jit_solution(1842000699996376410)
XLA Ops:
  0.6 3.7 %shard_map.120 = (bf16[1,1,512,256]{3,2,1,0:T(8,128)(2,1)}, bf16[512,512]{1,0:T(8,128)(2,1)}) custom-call(s32[1,512]{1,0:T(1,128)} %dec_hbm.1, s32[1,512]{1,0:T(1,128)} %enc_hbm.1, bf16[1,1,512,256]{3,2,1,0:T(8,128)(2,1)} %q_hbm.1, bf16[1,1,512,256]{3,2,1,0:T(8,128)(2,1)} %k_hbm.1, bf16[1,1,512,256]{3,2,1,0:T(8,128)(2,1)} %v_hbm.1, ...), custom_call_target="tpu_custom_call" | custom-call | flops 671088640 | bytes 2097152 | tf_op jit(solution)/shard_map/pallas_call | solution.py:40
  4.4 1.6 %copy-done.1 = bf16[1,4096,256]{2,1,0:T(8,128)(2,1)S(1)} copy-done((bf16[1,4096,256]{2,1,0:T(8,128)(2,1)S(1)}, bf16[1,4096,256]{2,1,0:T(8,128)(2,1)}, u32[]{:S(2)}) %copy-start.1) | copy-done | bytes 2097176
  8.4 4.1 %collective-permute-done.got_ref = bf16[4,2,512,256]{3,2,1,0:T(8,128)(2,1)S(1)} collective-permute-done((bf16[4,2,512,256]{3,2,1,0:T(8,128)(2,1)S(1)}, bf16[4,2,512,256]{3,2,1,0:T(8,128)(2,1)S(1)}, u32[]{:S(2)}, u32[]{:S(2)}) %collective-permute-start) | collective-permute-done | bytes 2097184 | tf_op jit(solution)/shard_map/ppermute | solution.py:286
  12.6 1.8 %shard_map.122 = (bf16[4,256,256]{2,1,0:T(8,128)(2,1)}, f32[4,256,256]{2,1,0:T(8,128)S(1)}, bf16[4,256,256]{2,1,0:T(8,128)(2,1)S(1)}, f32[4,256,256]{2,1,0:T(8,128)S(1)}) custom-call(bf16[512,512]{1,0:T(8,128)(2,1)S(1)} %get-tuple-element.26.both_ref.refs_10_.refs_8_, bf16[1,4096,256]{2,1,0:T(8,128)(2,1)S(1)} %copy-done, ...), custom_call_target="tpu_custom_call" | custom-call | flops 1073741824 | bytes 8388608 | tf_op jit(solution)/shard_map/pallas_call | solution.py:40
  18.3 1.8 %shard_map.124 = bf16[256,512]{1,0:T(8,128)(2,1)} custom-call(bf16[1,512,512]{2,1,0:T(8,128)(2,1)} %enc_ref.1), custom_call_target="tpu_custom_call" | custom-call | bytes 1048576 | tf_op jit(solution)/shard_map/pallas_call | solution.py:40
  20.1 1.7 %collective-permute-start.8 = (bf16[256,512]{1,0:T(8,128)(2,1)}, bf16[256,512]{1,0:T(8,128)(2,1)S(1)}, u32[]{:S(2)}, u32[]{:S(2)}) collective-permute-start(bf16[256,512]{1,0:T(8,128)(2,1)} %shard_map.124), channel_id=1, source_target_pairs={{0,0},{1,1},{2,2},{3,3},{4,130},{5,131},{6,128},{7,129},{128,6},{1... | collective-permute-start | bytes 786440 | tf_op jit(solution)/shard_map/ppermute | solution.py:303
  23.4 8.2 %collective-permute-start.19 = (bf16[512,512]{1,0:T(8,128)(2,1)S(1)}, bf16[512,512]{1,0:T(8,128)(2,1)S(1)}, u32[]{:S(2)}, u32[]{:S(2)}) collective-permute-start(bf16[512,512]{1,0:T(8,128)(2,1)S(1)} %get-tuple-element.26.both_ref.refs_10_.refs_8_), channel_id=1, source_target_pairs={{0,128},{128,0},{1,129},{129,1},{2,130},{130,2},{3,131},{131,3},{4... | collective-permute-start | bytes 1572872 | tf_op jit(solution)/shard_map/ppermute | solution.py:325
  33.1 13.9 %collective-permute-start.11 = (bf16[256,512]{1,0:T(8,128)(2,1)S(1)}, bf16[256,512]{1,0:T(8,128)(2,1)S(1)}, u32[]{:S(2)}, u32[]{:S(2)}) collective-permute-start(bf16[256,512]{1,0:T(8,128)(2,1)S(1)} %collective-permute-done.8.refs_0_), channel_id=1, source_target_pairs={{0,6},{1,7},{2,0},{3,1},{4,2},{5,3},{6,4},{7,5},{8,14},{9,15},{10,... | collective-permute-start | bytes 786440 | tf_op jit(solution)/shard_map/ppermute | solution.py:282
  48.5 10.6 %collective-permute-done.9.refs_3_ = bf16[256,512]{1,0:T(8,128)(2,1)S(1)} collective-permute-done((bf16[256,512]{1,0:T(8,128)(2,1)S(1)}, bf16[256,512]{1,0:T(8,128)(2,1)S(1)}, u32[]{:S(2)}, u32[]{:S(2)}) %collective-permute-start.9) | collective-permute-done | bytes 262176 | tf_op jit(solution)/shard_map/ppermute | solution.py:282
  59.4 2.1 %collective-permute-start.4 = (bf16[2,256,256]{2,1,0:T(8,128)(2,1)S(1)}, bf16[2,256,256]{2,1,0:T(8,128)(2,1)S(1)}, u32[]{:S(2)}, u32[]{:S(2)}) collective-permute-start(bf16[2,256,256]{2,1,0:T(8,128)(2,1)S(1)} %slice.60), channel_id=1, source_target_pairs={{0,16},{8,24},{16,0},{24,8},{32,48},{40,56},{48,32},{56,40},{64,80... | collective-permute-start | bytes 786440 | tf_op jit(solution)/shard_map/ppermute | solution.py:286
  61.5 6.3 %collective-permute-done.2 = bf16[2,256,256]{2,1,0:T(8,128)(2,1)S(1)} collective-permute-done((bf16[2,256,256]{2,1,0:T(8,128)(2,1)S(1)}, bf16[2,256,256]{2,1,0:T(8,128)(2,1)S(1)}, u32[]{:S(2)}, u32[]{:S(2)}) %collective-permute-start.2) | collective-permute-done | bytes 262176 | tf_op jit(solution)/shard_map/ppermute | solution.py:286
  68.8 3.5 %collective-permute-start.14 = (bf16[128,512]{1,0:T(8,128)(2,1)S(1)}, bf16[128,512]{1,0:T(8,128)(2,1)S(1)}, u32[]{:S(2)}, u32[]{:S(2)}) collective-permute-start(bf16[128,512]{1,0:T(8,128)(2,1)S(1)} %slice.53), channel_id=1, source_target_pairs={{0,6},{1,7},{2,0},{3,1},{4,2},{5,3},{6,4},{7,5},{8,14},{9,15},{10,... | collective-permute-start | bytes 393224 | tf_op jit(solution)/shard_map/ppermute | solution.py:282
  72.3 2.2 %collective-permute-start.10 = (bf16[256,512]{1,0:T(8,128)(2,1)S(1)}, bf16[256,512]{1,0:T(8,128)(2,1)S(1)}, u32[]{:S(2)}, u32[]{:S(2)}) collective-permute-start(bf16[256,512]{1,0:T(8,128)(2,1)S(1)} %collective-permute-done.9.refs_3_), channel_id=1, source_target_pairs={{0,1},{1,2},{2,3},{3,4},{4,5},{5,6},{6,7},{7,0},{8,9},{9,10},{10,1... | collective-permute-start | bytes 786440 | tf_op jit(solution)/shard_map/ppermute | solution.py:282
  77.6 5.7 %collective-permute-done.10.refs_0_ = bf16[256,512]{1,0:T(8,128)(2,1)S(1)} collective-permute-done((bf16[256,512]{1,0:T(8,128)(2,1)S(1)}, bf16[256,512]{1,0:T(8,128)(2,1)S(1)}, u32[]{:S(2)}, u32[]{:S(2)}) %collective-permute-start.10) | collective-permute-done | bytes 262176 | tf_op jit(solution)/shard_map/ppermute | solution.py:282
  85.9 5.7 %collective-permute-done.5.came_ref = bf16[512,256]{1,0:T(8,128)(2,1)S(1)} collective-permute-done((bf16[512,256]{1,0:T(8,128)(2,1)S(1)}, bf16[512,256]{1,0:T(8,128)(2,1)S(1)}, u32[]{:S(2)}, u32[]{:S(2)}) %collective-permute-start.5) | collective-permute-done | bytes 262176 | tf_op jit(solution)/shard_map/ppermute | solution.py:286
  93.1 1.8 %shard_map.125.refs_10_ = f32[2048,512]{1,0:T(8,128)S(1)} custom-call(bf16[256,512]{1,0:T(8,128)(2,1)S(1)} %collective-permute-done.8.refs_0_, bf16[256,512]{1,0:T(8,128)(2,1)S(1)} %collective-permute-done.20.refs_1_, bf16[256,512]{1,0:T(8,128)(2,1)S(1)} %collective-permute-done.21.refs_2_, bf16[256,512]{1,0:T(8,128)(2,1)S(1)} %collective-permute-done.9.refs_3_, ...), custom_call_target="tpu_custom_call" | custom-call | flops 1342177280 | bytes 8388608 | tf_op jit(solution)/shard_map/pallas_call | solution.py:40
  97.9 4.5 %collective-permute-done.27 = f32[8,256]{1,0:T(8,128)S(1)} collective-permute-done((f32[8,256]{1,0:T(8,128)S(1)}, f32[8,256]{1,0:T(8,128)S(1)}, u32[]{:S(2)}, u32[]{:S(2)}) %collective-permute-start.27) | collective-permute-done | bytes 8224 | tf_op jit(solution)/shard_map/ppermute | solution.py:386
  103.7 2.0 %collective-permute-start.29 = (f32[8,256]{1,0:T(8,128)S(1)}, f32[8,256]{1,0:T(8,128)S(1)}, u32[]{:S(2)}, u32[]{:S(2)}) collective-permute-start(f32[8,256]{1,0:T(8,128)S(1)} %add.19.square_ref), channel_id=1, source_target_pairs={{0,7},{1,0},{2,1},{3,2},{4,3},{5,4},{6,5},{7,6},{8,15},{9,8},{10,9... | collective-permute-start | bytes 24584 | tf_op jit(solution)/shard_map/ppermute | solution.py:282
  105.7 1.6 %collective-permute-done.28.behind_ref = f32[8,256]{1,0:T(8,128)S(1)} collective-permute-done((f32[8,256]{1,0:T(8,128)S(1)}, f32[8,256]{1,0:T(8,128)S(1)}, u32[]{:S(2)}, u32[]{:S(2)}) %collective-permute-start.28) | collective-permute-done | bytes 8224 | tf_op jit(solution)/shard_map/ppermute | solution.py:282
  107.4 2.7 %collective-permute-start.30 = (bf16[80,256]{1,0:T(8,128)(2,1)S(1)}, bf16[80,256]{1,0:T(8,128)(2,1)S(1)}, u32[]{:S(2)}, u32[]{:S(2)}) collective-permute-start(bf16[80,256]{1,0:T(8,128)(2,1)S(1)} %get-tuple-element.38), channel_id=1, source_target_pairs={{0,5},{1,6},{2,7},{3,0},{4,1},{5,2},{6,3},{7,4},{8,13},{9,14},{10,... | collective-permute-start | bytes 122888 | tf_op jit(solution)/shard_map/ppermute | solution.py:282
  110.1 1.7 %collective-permute-start.31 = (bf16[80,256]{1,0:T(8,128)(2,1)S(1)}, bf16[80,256]{1,0:T(8,128)(2,1)S(1)}, u32[]{:S(2)}, u32[]{:S(2)}) collective-permute-start(bf16[80,256]{1,0:T(8,128)(2,1)S(1)} %get-tuple-element.39), channel_id=1, source_target_pairs={{0,3},{1,4},{2,5},{3,6},{4,7},{5,0},{6,1},{7,2},{8,11},{9,12},{10,... | collective-permute-start | bytes 122888 | tf_op jit(solution)/shard_map/ppermute | solution.py:282
  111.8 2.0 %collective-permute-done.30.last_ref = bf16[80,256]{1,0:T(8,128)(2,1)S(1)} collective-permute-done((bf16[80,256]{1,0:T(8,128)(2,1)S(1)}, bf16[80,256]{1,0:T(8,128)(2,1)S(1)}, u32[]{:S(2)}, u32[]{:S(2)}) %collective-permute-start.30) | collective-permute-done | bytes 40992 | tf_op jit(solution)/shard_map/ppermute | solution.py:282
  113.8 4.2 %collective-permute-done.31.next_ref = bf16[80,256]{1,0:T(8,128)(2,1)S(1)} collective-permute-done((bf16[80,256]{1,0:T(8,128)(2,1)S(1)}, bf16[80,256]{1,0:T(8,128)(2,1)S(1)}, u32[]{:S(2)}, u32[]{:S(2)}) %collective-permute-start.31) | collective-permute-done | bytes 40992 | tf_op jit(solution)/shard_map/ppermute | solution.py:282
  118.0 2.2 %shard_map.128 = (f32[1,64,256]{2,1,0:T(8,128)}, f32[1,2048,256]{2,1,0:T(8,128)}, f32[1,2048,256]{2,1,0:T(8,128)}) custom-call(f32[64,256]{1,0:T(8,128)S(1)} %get-tuple-element.36.keep_ref, f32[8,256]{1,0:T(8,128)S(1)} %get-tuple-element.37.around_ref, bf16[80,256]{1,0:T(8,128)(2,1)S(1)} %collective-permute-done.30.last_ref, ...), custom_call_target="tpu_custom_call" | custom-call | bytes 8388608 | tf_op jit(solution)/shard_map/pallas_call | solution.py:40
  (77 shorter events, 23.7 us)
Async XLA Ops:
  17.1 29.8 %collective-permute-start.1 = (bf16[4,256,256]{2,1,0:T(8,128)(2,1)}, bf16[4,256,256]{2,1,0:T(8,128)(2,1)}, u32[]{:S(2)}, u32[]{:S(2)}) collective-permute-start(bf16[4,256,256]{2,1,0:T(8,128)(2,1)} %get-tuple-element.29), channel_id=1, source_target_pairs={{0,16},{8,24},{16,0},{24,8},{32,48},{40,56},{48,32},{56,40},{64,80... | collective-permute-start | bytes 1572872 | tf_op jit(solution)/shard_map/ppermute | solution.py:286
  20.1 11.5 %collective-permute-start.8 = (bf16[256,512]{1,0:T(8,128)(2,1)}, bf16[256,512]{1,0:T(8,128)(2,1)S(1)}, u32[]{:S(2)}, u32[]{:S(2)}) collective-permute-start(bf16[256,512]{1,0:T(8,128)(2,1)} %shard_map.124), channel_id=1, source_target_pairs={{0,0},{1,1},{2,2},{3,3},{4,130},{5,131},{6,128},{7,129},{128,6},{1... | collective-permute-start | bytes 786440 | tf_op jit(solution)/shard_map/ppermute | solution.py:303
  21.9 37.2 %collective-permute-start.3 = (bf16[4,256,256]{2,1,0:T(8,128)(2,1)}, bf16[4,256,256]{2,1,0:T(8,128)(2,1)S(1)}, u32[]{:S(2)}, u32[]{:S(2)}) collective-permute-start(bf16[4,256,256]{2,1,0:T(8,128)(2,1)} %copy-done.6), channel_id=1, source_target_pairs={{0,48},{8,56},{16,32},{24,40},{32,16},{40,24},{48,0},{56,8},{64,11... | collective-permute-start | bytes 1572872 | tf_op jit(solution)/shard_map/ppermute | solution.py:286
  23.4 35.9 %collective-permute-start.19 = (bf16[512,512]{1,0:T(8,128)(2,1)S(1)}, bf16[512,512]{1,0:T(8,128)(2,1)S(1)}, u32[]{:S(2)}, u32[]{:S(2)}) collective-permute-start(bf16[512,512]{1,0:T(8,128)(2,1)S(1)} %get-tuple-element.26.both_ref.refs_10_.refs_8_), channel_id=1, source_target_pairs={{0,128},{128,0},{1,129},{129,1},{2,130},{130,2},{3,131},{131,3},{4... | collective-permute-start | bytes 1572872 | tf_op jit(solution)/shard_map/ppermute | solution.py:325
  31.6 27.4 %collective-permute-start.9 = (bf16[256,512]{1,0:T(8,128)(2,1)S(1)}, bf16[256,512]{1,0:T(8,128)(2,1)S(1)}, u32[]{:S(2)}, u32[]{:S(2)}) collective-permute-start(bf16[256,512]{1,0:T(8,128)(2,1)S(1)} %collective-permute-done.8.refs_0_), channel_id=1, source_target_pairs={{0,2},{1,3},{2,4},{3,5},{4,6},{5,7},{6,0},{7,1},{8,10},{9,11},{10,... | collective-permute-start | bytes 786440 | tf_op jit(solution)/shard_map/ppermute | solution.py:282
  33.1 26.0 %collective-permute-start.11 = (bf16[256,512]{1,0:T(8,128)(2,1)S(1)}, bf16[256,512]{1,0:T(8,128)(2,1)S(1)}, u32[]{:S(2)}, u32[]{:S(2)}) collective-permute-start(bf16[256,512]{1,0:T(8,128)(2,1)S(1)} %collective-permute-done.8.refs_0_), channel_id=1, source_target_pairs={{0,6},{1,7},{2,0},{3,1},{4,2},{5,3},{6,4},{7,5},{8,14},{9,15},{10,... | collective-permute-start | bytes 786440 | tf_op jit(solution)/shard_map/ppermute | solution.py:282
  47.0 21.8 %collective-permute-start.20 = (bf16[256,512]{1,0:T(8,128)(2,1)S(1)}, bf16[256,512]{1,0:T(8,128)(2,1)S(1)}, u32[]{:S(2)}, u32[]{:S(2)}) collective-permute-start(bf16[256,512]{1,0:T(8,128)(2,1)S(1)} %collective-permute-done.8.refs_0_), channel_id=1, source_target_pairs={{0,1},{1,2},{2,3},{3,4},{4,5},{5,6},{6,7},{7,0},{8,9},{9,10},{10,1... | collective-permute-start | bytes 786440 | tf_op jit(solution)/shard_map/ppermute | solution.py:282
  59.1 13.2 %collective-permute-start.21 = (bf16[256,512]{1,0:T(8,128)(2,1)S(1)}, bf16[256,512]{1,0:T(8,128)(2,1)S(1)}, u32[]{:S(2)}, u32[]{:S(2)}) collective-permute-start(bf16[256,512]{1,0:T(8,128)(2,1)S(1)} %collective-permute-done.8.refs_0_), channel_id=1, source_target_pairs={{0,7},{1,0},{2,1},{3,2},{4,3},{5,4},{6,5},{7,6},{8,15},{9,8},{10,9... | collective-permute-start | bytes 786440 | tf_op jit(solution)/shard_map/ppermute | solution.py:282
  59.1 15.4 %collective-permute-start.22 = (bf16[256,512]{1,0:T(8,128)(2,1)S(1)}, bf16[256,512]{1,0:T(8,128)(2,1)S(1)}, u32[]{:S(2)}, u32[]{:S(2)}) collective-permute-start(bf16[256,512]{1,0:T(8,128)(2,1)S(1)} %collective-permute-done.8.refs_0_), channel_id=1, source_target_pairs={{0,8},{8,0},{16,24},{24,16},{32,40},{40,32},{48,56},{56,48},{64,72... | collective-permute-start | bytes 786440 | tf_op jit(solution)/shard_map/ppermute | solution.py:286
  59.1 8.7 %collective-permute-start.2 = (bf16[2,256,256]{2,1,0:T(8,128)(2,1)S(1)}, bf16[2,256,256]{2,1,0:T(8,128)(2,1)S(1)}, u32[]{:S(2)}, u32[]{:S(2)}) collective-permute-start(bf16[2,256,256]{2,1,0:T(8,128)(2,1)S(1)} %slice.61), channel_id=1, source_target_pairs={{0,48},{8,56},{16,32},{24,40},{32,16},{40,24},{48,0},{56,8},{64,11... | collective-permute-start | bytes 786440 | tf_op jit(solution)/shard_map/ppermute | solution.py:286
  59.4 16.1 %collective-permute-start.4 = (bf16[2,256,256]{2,1,0:T(8,128)(2,1)S(1)}, bf16[2,256,256]{2,1,0:T(8,128)(2,1)S(1)}, u32[]{:S(2)}, u32[]{:S(2)}) collective-permute-start(bf16[2,256,256]{2,1,0:T(8,128)(2,1)S(1)} %slice.60), channel_id=1, source_target_pairs={{0,16},{8,24},{16,0},{24,8},{32,48},{40,56},{48,32},{56,40},{64,80... | collective-permute-start | bytes 786440 | tf_op jit(solution)/shard_map/ppermute | solution.py:286
  68.8 8.8 %collective-permute-start.14 = (bf16[128,512]{1,0:T(8,128)(2,1)S(1)}, bf16[128,512]{1,0:T(8,128)(2,1)S(1)}, u32[]{:S(2)}, u32[]{:S(2)}) collective-permute-start(bf16[128,512]{1,0:T(8,128)(2,1)S(1)} %slice.53), channel_id=1, source_target_pairs={{0,6},{1,7},{2,0},{3,1},{4,2},{5,3},{6,4},{7,5},{8,14},{9,15},{10,... | collective-permute-start | bytes 393224 | tf_op jit(solution)/shard_map/ppermute | solution.py:282
  72.3 11.1 %collective-permute-start.10 = (bf16[256,512]{1,0:T(8,128)(2,1)S(1)}, bf16[256,512]{1,0:T(8,128)(2,1)S(1)}, u32[]{:S(2)}, u32[]{:S(2)}) collective-permute-start(bf16[256,512]{1,0:T(8,128)(2,1)S(1)} %collective-permute-done.9.refs_3_), channel_id=1, source_target_pairs={{0,1},{1,2},{2,3},{3,4},{4,5},{5,6},{6,7},{7,0},{8,9},{9,10},{10,1... | collective-permute-start | bytes 786440 | tf_op jit(solution)/shard_map/ppermute | solution.py:282
  74.4 10.4 %collective-permute-start.12 = (bf16[256,512]{1,0:T(8,128)(2,1)S(1)}, bf16[256,512]{1,0:T(8,128)(2,1)S(1)}, u32[]{:S(2)}, u32[]{:S(2)}) collective-permute-start(bf16[256,512]{1,0:T(8,128)(2,1)S(1)} %collective-permute-done.11.refs_4_), channel_id=1, source_target_pairs={{0,7},{1,0},{2,1},{3,2},{4,3},{5,4},{6,5},{7,6},{8,15},{9,8},{10,9... | collective-permute-start | bytes 786440 | tf_op jit(solution)/shard_map/ppermute | solution.py:282
  75.5 9.4 %collective-permute-start.23 = (bf16[256,512]{1,0:T(8,128)(2,1)S(1)}, bf16[256,512]{1,0:T(8,128)(2,1)S(1)}, u32[]{:S(2)}, u32[]{:S(2)}) collective-permute-start(bf16[256,512]{1,0:T(8,128)(2,1)S(1)} %collective-permute-done.20.refs_1_), channel_id=1, source_target_pairs={{0,8},{8,0},{16,24},{24,16},{32,40},{40,32},{48,56},{56,48},{64,72... | collective-permute-start | bytes 786440 | tf_op jit(solution)/shard_map/ppermute | solution.py:286
  75.5 9.9 %collective-permute-start.24 = (bf16[256,512]{1,0:T(8,128)(2,1)S(1)}, bf16[256,512]{1,0:T(8,128)(2,1)S(1)}, u32[]{:S(2)}, u32[]{:S(2)}) collective-permute-start(bf16[256,512]{1,0:T(8,128)(2,1)S(1)} %collective-permute-done.21.refs_2_), channel_id=1, source_target_pairs={{0,8},{8,0},{16,24},{24,16},{32,40},{40,32},{48,56},{56,48},{64,72... | collective-permute-start | bytes 786440 | tf_op jit(solution)/shard_map/ppermute | solution.py:286
  77.6 7.9 %collective-permute-start.25 = (bf16[256,512]{1,0:T(8,128)(2,1)S(1)}, bf16[256,512]{1,0:T(8,128)(2,1)S(1)}, u32[]{:S(2)}, u32[]{:S(2)}) collective-permute-start(bf16[256,512]{1,0:T(8,128)(2,1)S(1)} %collective-permute-done.9.refs_3_), channel_id=1, source_target_pairs={{0,8},{8,0},{16,24},{24,16},{32,40},{40,32},{48,56},{56,48},{64,72... | collective-permute-start | bytes 786440 | tf_op jit(solution)/shard_map/ppermute | solution.py:286
  83.3 8.2 %collective-permute-start.5 = (bf16[512,256]{1,0:T(8,128)(2,1)S(1)}, bf16[512,256]{1,0:T(8,128)(2,1)S(1)}, u32[]{:S(2)}, u32[]{:S(2)}) collective-permute-start(bf16[512,256]{1,0:T(8,128)(2,1)S(1)} %maximum_bitcast_fusion), channel_id=1, source_target_pairs={{0,64},{8,72},{16,80},{24,88},{32,96},{40,104},{48,112},{56,120},{... | collective-permute-start | bytes 786440 | tf_op jit(solution)/shard_map/ppermute | solution.py:286
  84.9 10.9 %collective-permute-start.15 = (bf16[256,512]{1,0:T(8,128)(2,1)S(1)}, bf16[256,512]{1,0:T(8,128)(2,1)S(1)}, u32[]{:S(2)}, u32[]{:S(2)}) collective-permute-start(bf16[256,512]{1,0:T(8,128)(2,1)S(1)} %collective-permute-done.10.refs_0_), channel_id=1, source_target_pairs={{0,8},{8,0},{16,24},{24,16},{32,40},{40,32},{48,56},{56,48},{64,72... | collective-permute-start | bytes 786440 | tf_op jit(solution)/shard_map/ppermute | solution.py:286
  85.4 10.4 %collective-permute-start.16 = (bf16[256,512]{1,0:T(8,128)(2,1)S(1)}, bf16[256,512]{1,0:T(8,128)(2,1)S(1)}, u32[]{:S(2)}, u32[]{:S(2)}) collective-permute-start(bf16[256,512]{1,0:T(8,128)(2,1)S(1)} %collective-permute-done.12.refs_1_), channel_id=1, source_target_pairs={{0,8},{8,0},{16,24},{24,16},{32,40},{40,32},{48,56},{56,48},{64,72... | collective-permute-start | bytes 786440 | tf_op jit(solution)/shard_map/ppermute | solution.py:286
  85.5 9.4 %collective-permute-start.17 = (bf16[128,512]{1,0:T(8,128)(2,1)S(1)}, bf16[128,512]{1,0:T(8,128)(2,1)S(1)}, u32[]{:S(2)}, u32[]{:S(2)}) collective-permute-start(bf16[128,512]{1,0:T(8,128)(2,1)S(1)} %collective-permute-done.13.refs_2_), channel_id=1, source_target_pairs={{0,8},{8,0},{16,24},{24,16},{32,40},{40,32},{48,56},{56,48},{64,72... | collective-permute-start | bytes 393224 | tf_op jit(solution)/shard_map/ppermute | solution.py:286
  91.7 15.6 %collective-permute-start.7 = (bf16[192,256]{1,0:T(8,128)(2,1)S(1)}, bf16[192,256]{1,0:T(8,128)(2,1)S(1)}, u32[]{:S(2)}, u32[]{:S(2)}) collective-permute-start(bf16[192,256]{1,0:T(8,128)(2,1)S(1)} %get-tuple-element.34), channel_id=1, source_target_pairs={{0,7},{1,0},{2,1},{3,2},{4,3},{5,4},{6,5},{7,6},{8,15},{9,8},{10,9... | collective-permute-start | bytes 294920 | tf_op jit(solution)/shard_map/ppermute | solution.py:282
  94.9 12.4 %collective-permute-start.6 = (bf16[128,256]{1,0:T(8,128)(2,1)S(1)}, bf16[128,256]{1,0:T(8,128)(2,1)S(1)}, u32[]{:S(2)}, u32[]{:S(2)}) collective-permute-start(bf16[128,256]{1,0:T(8,128)(2,1)S(1)} %get-tuple-element.33), channel_id=1, source_target_pairs={{0,1},{1,2},{2,3},{3,4},{4,5},{5,6},{6,7},{7,0},{8,9},{9,10},{10,1... | collective-permute-start | bytes 196616 | tf_op jit(solution)/shard_map/ppermute | solution.py:282
  110.1 7.8 %collective-permute-start.31 = (bf16[80,256]{1,0:T(8,128)(2,1)S(1)}, bf16[80,256]{1,0:T(8,128)(2,1)S(1)}, u32[]{:S(2)}, u32[]{:S(2)}) collective-permute-start(bf16[80,256]{1,0:T(8,128)(2,1)S(1)} %get-tuple-element.39), channel_id=1, source_target_pairs={{0,3},{1,4},{2,5},{3,6},{4,7},{5,0},{6,1},{7,2},{8,11},{9,12},{10,... | collective-permute-start | bytes 122888 | tf_op jit(solution)/shard_map/ppermute | solution.py:282
  (15 other events, 91.3 us)
